TPU v7x, 32 devices: a whole 2x2x4 slice. The times are simulated.
32 devices in a mesh: section: 8 (over y, x, core), rep: 4 (over z).
Axes of the slice: x: 2, y: 2, z: 4, core: 2. Of those that a mesh axis runs over, the one named last changes fastest.
Arguments:
- features: bfloat16 [16384, 128], P('section'), may hold values from -6 to 6
- order: int32 [16384], P('section'), may hold values from 0 to 2047, as said below
- tiles: bfloat16 [8, 4, 2, 96, 128, 128], P('section', 'rep'), may hold values from -0.125 to 0.125
- tile_rows: int32 [8, 4, 2, 96], P('section', 'rep'), may hold values from 0 to 15, as said below
- tile_cols: int32 [8, 4, 2, 96], P('section', 'rep'), may hold values from 0 to 15, as said below
- live: int32 [8, 4, 2], P('section', 'rep'), may hold values from 1 to 96, as said below
- weight: bfloat16 [128, 128], replicated, may hold values from -0.5 to 0.5
- cotangent: bfloat16 [16384, 128], P('section'), may hold values from -6 to 6
Outputs:
- hidden: bfloat16 [16384, 128], P('section')
- weight_grad: float32 [128, 128], replicated
- feature_grad: bfloat16 [16384, 128], P('section')
Inputs may be any that keep to these rules, and one draw needn't show every extreme that they name: `order`: within each panel of 2048 rows, a permutation of the local row numbers. For one section, replica and round, the 96 pairs (tile_rows, tile_cols) are distinct. `tile_cols`: block column within the panel j * 4 + r for replica r and round j. Some section, replica and round has all 96 slots live.
All inputs are finite; a program needn't handle non-finite values.
Results may differ from a plain program's by a relative error of at most 0.012.
Values may be sent and summed in bfloat16 or wider, within the bound.
No kernel may reach another device: no remote copies, remote signals or barrier semaphores. Data moves between devices by JAX's collectives and lax.ppermute only.
A program may use at most 192 MiB of HBM per device.

v0:
```python
import math
import jax
import jax.numpy as jnp
from jax import lax
from jax.sharding import PartitionSpec as P


def spread(value, axis, source):
    kept = jnp.where(lax.axis_index(axis) == source, value, 0).astype(value.dtype)
    return lax.psum(kept, axis)


def shards(features, order, tiles, tile_rows, tile_cols, live, weight, cotangent):
    rep_count = lax.axis_size("rep")
    section_count = lax.axis_size("section")
    rep_index = lax.axis_index("rep")
    section_index = lax.axis_index("section")
    panel_rows, width = features.shape
    block_rows = tiles.shape[-1]
    blocks = panel_rows // block_rows
    rounds = tiles.shape[2]
    slot_count = tiles.shape[3]
    own_tiles = tiles[0, 0]
    row_table = tile_rows[0, 0]
    col_table = tile_cols[0, 0]
    live_counts = live[0, 0]
    slot_ids = jnp.arange(slot_count, dtype=jnp.int32)
    block_ids = jnp.arange(blocks, dtype=jnp.int32)
    grad_scale = 1.0 / math.sqrt(panel_rows * section_count)
    reordered = jnp.take(features, order, axis=0)

    def forward_round(round_no, running):
        root = round_no * rep_count + rep_index
        panel = spread(reordered, "section", root)
        tile_set = lax.dynamic_index_in_dim(own_tiles, round_no, 0, keepdims=False)
        row_ids = lax.dynamic_index_in_dim(row_table, round_no, 0, keepdims=False)
        col_ids = lax.dynamic_index_in_dim(col_table, round_no, 0, keepdims=False)
        count_now = lax.dynamic_index_in_dim(live_counts, round_no, 0, keepdims=False)
        picked = jnp.take(panel.reshape(blocks, block_rows, width), col_ids, axis=0)
        products = jnp.einsum("kab,kbf->kaf", tile_set, picked, preferred_element_type=jnp.float32)
        select = (
            (row_ids[None, :] == block_ids[:, None]) & (slot_ids < count_now)[None, :]
        ).astype(jnp.float32)
        return running + jnp.einsum(
            "pk,kaf->paf", select, products, precision=lax.Precision.HIGHEST
        )

    partial_sum = lax.fori_loop(
        0, rounds, forward_round, jnp.zeros((blocks, block_rows, width), jnp.float32)
    )
    partial_sum = partial_sum.reshape(panel_rows, width)
    share_rows = panel_rows // rep_count
    row_share = lax.psum_scatter(partial_sum, "rep", scatter_dimension=0, tiled=True)
    co_share = lax.dynamic_slice_in_dim(cotangent, rep_index * share_rows, share_rows, 0)
    aggregated = row_share.astype(jnp.bfloat16)
    preact = jnp.dot(aggregated, weight, preferred_element_type=jnp.float32)
    out_rows = jax.nn.silu(preact).astype(jnp.bfloat16)
    sigmoid_part = jax.nn.sigmoid(preact)
    grad_pre = (
        co_share.astype(jnp.float32) * sigmoid_part * (1.0 + preact * (1.0 - sigmoid_part))
    ).astype(jnp.bfloat16)
    grad_part = jnp.einsum("nf,ng->fg", aggregated, grad_pre, preferred_element_type=jnp.float32)
    up_rows = jnp.einsum("ng,fg->nf", grad_pre, weight, preferred_element_type=jnp.float32).astype(
        jnp.bfloat16
    )
    hidden_share, grad_part, upstream_share = (out_rows, grad_part, up_rows)
    weight_grad = lax.psum(grad_part, ("section", "rep")) * grad_scale
    hidden, upstream = (
        lax.all_gather(hidden_share, "rep", axis=0, tiled=True),
        lax.all_gather(upstream_share, "rep", axis=0, tiled=True),
    )
    up_blocks = upstream.reshape(blocks, block_rows, width)
    picked_up = jnp.take(up_blocks, row_table.reshape(-1), axis=0).reshape(
        rounds, slot_count, block_rows, width
    )
    products_back = jnp.einsum(
        "jkab,jkaf->jkbf", own_tiles, picked_up, preferred_element_type=jnp.float32
    )
    alive_mask = slot_ids[None, None, :] < live_counts[:, None, None]
    select_back = ((col_table[:, None, :] == block_ids[None, :, None]) & alive_mask).astype(
        jnp.float32
    )
    contrib = jnp.einsum(
        "jpk,jkbf->jpbf", select_back, products_back, precision=lax.Precision.HIGHEST
    )
    contrib = lax.optimization_barrier(contrib.astype(jnp.bfloat16)).astype(jnp.float32)
    contrib = contrib.reshape(rounds, panel_rows, width)
    totals = lax.psum(contrib.astype(jnp.bfloat16), "section").astype(jnp.float32)
    own_panel = lax.dynamic_index_in_dim(
        totals, section_index // rep_count, 0, keepdims=False
    ).astype(jnp.bfloat16)
    grad_rows = spread(own_panel, "rep", section_index % rep_count)
    feature_grad = jnp.zeros_like(features).at[order].set(grad_rows)
    return (hidden, weight_grad, feature_grad)


def solution(mesh):
    placed = (
        P("section", None),
        P("section"),
        P("section", "rep", None, None, None, None),
        P("section", "rep", None, None),
        P("section", "rep", None, None),
        P("section", "rep", None),
        P(),
        P("section", None),
    )
    return jax.shard_map(
        shards,
        mesh=mesh,
        in_specs=placed,
        out_specs=(P("section", None), P(), P("section", None)),
        check_vma=False,
    )
```

profile of v0, /device:TPU:0, one launch (start us, length us, event | category | flops | bytes accessed | tf_op | source)
XLA Modules:
  0.0 487.0 jit_solution(13288153377587932532)
XLA Ops:
  8.0 0.0 copy-start
  8.0 0.8 compare_select_fusion.2
  8.8 0.7 compare_and_fusion.1
  9.5 0.0 copy-done
  9.5 6.2 %gather_fusion.1 = bf16[2048,128]{1,0:T(8,128)(2,1)S(1)} fusion(bf16[2048,128]{1,0:T(8,128)(2,1)S(1)} %copy-done, s32[2048]{0:T(1024)S(1)} %get-tuple-element.296), kind=kCustom, calls=%fused_computation.1 | custom fusion | bytes 1056768 | tf_op jit(solution)/shard_map/jit(_take)/gather | solution.py:30
  15.7 0.3 broadcast_select_fusion.1
  16.0 0.0 copy-start.2
  16.0 147.6 %while.16 = (s32[]{:T(128)}, f32[16,128,128]{2,0,1:T(8,128)S(1)}, s32[2,96]{1,0:T(2,128)}, s32[2]{0:T(128)}, bf16[2,96,128,128]{3,2,1,0:T(8,128)(2,1)}, /*index=...) while((s32[]{:T(128)}, f32[16,128,128]{2,0,1:T(8,128)S(1)}, ...), condition=%wide.region_2.3_spmd.clone, body=%wide.region_0.0_spmd.clone.sunk | while | flops 707269568 | bytes 31465112 | solution.py:48
  16.0 0.0 all-reduce.11.cloned.1.call-start
  16.1 0.8 broadcast_select_fusion.3
  16.9 0.0 all-reduce.11.cloned.1.call-update
  17.0 0.7 fusion.64
  17.7 0.7 compare_and_fusion.4
  18.3 1.2 dynamic_slice.80
  19.6 0.6 iota_compare_fusion.5
  20.2 0.7 fusion.66
  20.9 57.2 %all-reduce.11.cloned.1.call-done = bf16[16,128,128]{2,1,0:T(8,128)(2,1)} async-done(((bf16[16,128,128]{2,1,0:T(8,128)(2,1)}), bf16[16,128,128]{2,1,0:T(8,128)(2,1)}) %all-reduce.11.cloned.1.call-update) | async-done | bytes 524304 | tf_op jit(solution)/shard_map/while/body/eval_jaxpr/psum | solution.py:10
  78.1 3.7 gather_fusion
  81.9 3.9 fusion.65
  85.8 5.7 %fusion.67 = f32[16,128,128]{2,0,1:T(8,128)S(1)} fusion(f32[96,128,128]{2,1,0:T(8,128)S(1)} %fusion.65, f32[16,128,128]{2,0,1:T(8,128)S(1)} %get-tuple-element.360, pred[]{:T(512)S(6)} %compare.6, s32[96]{0:T(128)S(1)} %fusion.66, pred[96]{0:T(512)(128)(4,1)S(1)} %iota_compare_fusion.5), kind=kOutput, calls=%fused_computation.14.clone.1 | convolution fusion | flops 302517248 | bytes 8389089 | tf_op jit(solution)/shard_map/while/body/eval_jaxpr/pk,kaf->paf/dot_general | solution.py:44
  91.5 0.0 all-reduce.11.cloned.1.call-start
  91.6 0.8 broadcast_select_fusion.3
  92.4 0.0 all-reduce.11.cloned.1.call-update
  92.4 0.7 fusion.64
  93.1 0.7 compare_and_fusion.4
  93.8 1.2 dynamic_slice.80
  95.1 0.6 iota_compare_fusion.5
  95.7 0.7 fusion.66
  96.4 53.8 %all-reduce.11.cloned.1.call-done = bf16[16,128,128]{2,1,0:T(8,128)(2,1)} async-done(((bf16[16,128,128]{2,1,0:T(8,128)(2,1)}), bf16[16,128,128]{2,1,0:T(8,128)(2,1)}) %all-reduce.11.cloned.1.call-update) | async-done | bytes 524304 | tf_op jit(solution)/shard_map/while/body/eval_jaxpr/psum | solution.py:10
  150.2 3.7 gather_fusion
  154.0 3.9 fusion.65
  157.9 5.7 %fusion.67 = f32[16,128,128]{2,0,1:T(8,128)S(1)} fusion(f32[96,128,128]{2,1,0:T(8,128)S(1)} %fusion.65, f32[16,128,128]{2,0,1:T(8,128)S(1)} %get-tuple-element.360, pred[]{:T(512)S(6)} %compare.6, s32[96]{0:T(128)S(1)} %fusion.66, pred[96]{0:T(512)(128)(4,1)S(1)} %iota_compare_fusion.5), kind=kOutput, calls=%fused_computation.14.clone.1 | convolution fusion | flops 302517248 | bytes 8389089 | tf_op jit(solution)/shard_map/while/body/eval_jaxpr/pk,kaf->paf/dot_general | solution.py:44
  163.6 0.0 reduce-scatter.2.cloned.1.call-start
  163.7 1.3 copy.11
  165.0 0.0 reduce-scatter.2.cloned.1.call-update
  165.0 0.0 all-reduce.7.cloned.1.call-start
  165.1 0.8 reshape_squeeze.3
  165.8 0.7 iota_compare_fusion.3
  166.6 0.7 compare_and_fusion.2
  167.3 25.6 %reduce-scatter.2.cloned.1.call-done = f32[512,128]{1,0:T(8,128)} async-done(((f32[2048,128]{1,0:T(8,128)}), f32[512,128]{1,0:T(8,128)}) %reduce-scatter.2.cloned.1.call-update) | async-done | bytes 262160 | tf_op jit(solution)/shard_map/reduce_scatter | solution.py:53
  192.9 0.0 copy-done.2
  192.9 1.3 multiply_convert_fusion
  194.2 0.2 convolution_convert_fusion
  194.3 16.2 %all_gather.7 = bf16[2048,128]{1,0:T(8,128)(2,1)S(1)} all-gather(bf16[512,128]{1,0:T(8,128)(2,1)S(1)} %convolution_convert_fusion), channel_id=1, replica_groups=mesh['section'=8,'rep'=4] {'rep'}, dimensions={0}, use_global_device_ids=true | all-gather | bytes 655360 | tf_op jit(solution)/shard_map/all_gather | solution.py:70
  210.5 8.0 %gather_fusion.2 = bf16[192,128,128]{2,1,0:T(8,128)(2,1)} fusion(bf16[16,128,128]{2,1,0:T(8,128)(2,1)S(1)} %bitcast.60, s32[1024]{0:T(1024)S(1)} %pad_clamp_fusion.1), kind=kCustom, calls=%fused_computation.2 | custom fusion | bytes 12583680 | tf_op jit(solution)/shard_map/jit(_take)/gather | solution.py:73
  218.5 11.6 %fusion.26 = f32[2,96,128,128]{3,2,1,0:T(8,128)} fusion(bf16[2,96,128,128]{3,2,1,0:T(8,128)(2,1)} %bitcast.64, pred[2,96]{1,0:T(4,128)(4,1)S(1)} %compare_and_fusion.2, bf16[1,1,2,96,128,128]{5,4,3,2,1,0:T(8,128)(2,1)} %bitcast.62), kind=kOutput, calls=%fused_computation.34 | convolution fusion | flops 808452096 | bytes 25166016 | tf_op jit(solution)/shard_map/jkab,jkaf->jkbf/dot_general | solution.py:76
  230.1 12.8 %copy.14 = f32[2,96,128,128]{2,1,3,0:T(8,128)} copy(f32[2,96,128,128]{3,2,1,0:T(8,128)} %fusion.26) | data formatting | bytes 25165824 | tf_op jit(solution)/shard_map/jkab,jkaf->jkbf/dot_general | solution.py:76
  242.8 0.0 copy-done.3
  242.8 7.2 %fusion.30 = bf16[2,16,128,128]{3,1,2,0:T(8,128)(2,1)S(1)} fusion(f32[2,96,128,128]{2,1,3,0:T(8,128)} %copy.14, s32[2,96]{1,0:T(2,128)S(1)} %copy-done.3, pred[2,96]{1,0:T(4,128)(4,1)S(1)} %iota_compare_fusion.3), kind=kOutput, calls=%fused_computation.38 | convolution fusion | flops 604510208 | bytes 13632448 | tf_op jit(solution)/shard_map/jpk,jkbf->jpbf/dot_general | solution.py:83
  250.1 1.3 copy.12
  251.4 0.0 all-reduce.7.cloned.1.call-update
  251.4 0.0 all-reduce.5.cloned.1.call-start
  251.5 0.9 fusion.37
  252.4 0.0 all-reduce.5.cloned.1.call-update
  252.4 0.0 all-reduce.9.cloned.1.call-start
  252.5 53.3 %all-reduce.7.cloned.1.call-done = bf16[2,2048,128]{2,1,0:T(8,128)(2,1)} async-done(((bf16[2,2048,128]{2,1,0:T(8,128)(2,1)}), bf16[2,2048,128]{2,1,0:T(8,128)(2,1)}) %all-reduce.7.cloned.1.call-update) | async-done | bytes 1048592 | tf_op jit(solution)/shard_map/psum | solution.py:88
  305.8 1.9 fusion.34
  307.7 0.0 all-reduce.9.cloned.1.call-update
  307.7 14.8 %all_gather.6 = bf16[2048,128]{1,0:T(8,128)(2,1)S(1)} all-gather(bf16[512,128]{1,0:T(8,128)(2,1)S(1)} %get-tuple-element.294), channel_id=1, replica_groups=mesh['section'=8,'rep'=4] {'rep'}, dimensions={0}, use_global_device_ids=true | all-gather | bytes 655360 | tf_op jit(solution)/shard_map/all_gather | solution.py:69
  322.5 106.7 %all-reduce.5.cloned.1.call-done = f32[128,128]{1,0:T(8,128)} async-done(((f32[128,128]{1,0:T(8,128)}), f32[128,128]{1,0:T(8,128)}) %all-reduce.5.cloned.1.call-update) | async-done | bytes 65552 | tf_op jit(solution)/shard_map/psum | solution.py:67
  429.3 1.5 broadcast_multiply_fusion
  430.7 41.1 %all-reduce.9.cloned.1.call-done = bf16[2048,128]{1,0:T(8,128)(2,1)} async-done(((bf16[2048,128]{1,0:T(8,128)(2,1)}), bf16[2048,128]{1,0:T(8,128)(2,1)}) %all-reduce.9.cloned.1.call-update) | async-done | bytes 524304 | tf_op jit(solution)/shard_map/psum | solution.py:10
  471.8 6.8 %scatter_custom_fusion = bf16[2048,128]{1,0:T(8,128)(2,1)} fusion(s32[2048]{0:T(1024)S(1)} %get-tuple-element.295, bf16[2048,128]{1,0:T(8,128)(2,1)} %all-reduce.9.cloned.1.call-done, bf16[]{:T(256)} %constant.190.clone.1), kind=kCustom, calls=%fused_computation.44 | custom fusion | bytes 524800 | tf_op jit(solution)/shard_map/scatter | solution.py:93
  478.7 0.8 copy.33
  (8 shorter events, 0.0 us)
Async XLA Ops:
  8.0 1.5 copy-start
  16.0 176.9 %copy-start.2 = (bf16[128,128]{1,0:T(8,128)(2,1)S(1)}, bf16[128,128]{1,0:T(8,128)(2,1)}, u32[]{:S(2)}) copy-start(bf16[128,128]{1,0:T(8,128)(2,1)} %param.16) | copy-start | bytes 98308
  16.0 62.1 %all-reduce.11.cloned.1.call-start = ((), (), s32[]{:S(2)}) async-start(), calls=%async_computation.5 | async-start | bytes 1048576 | tf_op jit(solution)/shard_map/while/body/eval_jaxpr/psum | solution.py:10
  91.5 58.7 %all-reduce.11.cloned.1.call-start = ((), (), s32[]{:S(2)}) async-start(), calls=%async_computation.5 | async-start | bytes 1048576 | tf_op jit(solution)/shard_map/while/body/eval_jaxpr/psum | solution.py:10
  163.6 29.2 %reduce-scatter.2.cloned.1.call-start = ((), (), s32[]{:S(2)}) async-start(), calls=%async_computation.1 | async-start | bytes 1310720 | tf_op jit(solution)/shard_map/reduce_scatter | solution.py:53
  165.0 140.7 %all-reduce.7.cloned.1.call-start = ((), (), s32[]{:S(2)}) async-start(), calls=%async_computation.3 | async-start | bytes 2097152 | tf_op jit(solution)/shard_map/psum | solution.py:88
  230.1 12.8 %copy-start.3 = (s32[2,96]{1,0:T(2,128)S(1)}, s32[2,96]{1,0:T(2,128)}, u32[]{:S(2)}) copy-start(s32[2,96]{1,0:T(2,128)} %get-tuple-element.411) | copy-start | bytes 2308
  242.8 8.7 %copy-start.1 = (f32[512,128]{1,0:T(8,128)S(1)}, f32[512,128]{1,0:T(8,128)}, u32[]{:S(2)}) copy-start(f32[512,128]{1,0:T(8,128)} %reduce-scatter.2.cloned.1.call-done) | copy-start | bytes 786436
  251.4 177.8 %all-reduce.5.cloned.1.call-start = ((), (), s32[]{:S(2)}) async-start(), calls=%async_computation.2 | async-start | bytes 131072 | tf_op jit(solution)/shard_map/psum | solution.py:67
  252.4 219.4 %all-reduce.9.cloned.1.call-start = ((), (), s32[]{:S(2)}) async-start(), calls=%async_computation.4 | async-start | bytes 1048576 | tf_op jit(solution)/shard_map/psum | solution.py:10
Sparse Core Ops, SparseCore 0:
  20.8 57.2 all-reduce.10
  96.3 53.8 all-reduce.10
Sparse Core Ops, SparseCore 1:
  166.4 26.4 reduce-scatter.1
  251.5 54.2 all-reduce.6
  312.7 116.5 all-reduce.4
  432.3 39.4 all-reduce.8
where the time goes:
time: 488 us; the launch traced here: 487 us
  waiting for transfers between devices  338 us (69%)
  local copies, waits for them, and re-layouts  49.3 us (10%)
  matrix products  40.4 us (8%)
  blocking collectives  31 us (6%)
  between operations  15.8 us (3%)
  other arithmetic  12.4 us (3%)
    psum x3, waiting for transfers between devices, spread(): return lax.psum(kept, axis)  152 us
    psum x1, waiting for transfers between devices, shards(): weight_grad = lax.psum(grad_part, ('section', 'rep')) * grad_scale  107 us
    psum x1, waiting for transfers between devices, shards(): lax.psum(contrib.astype(jnp.bfloat16), 'section').astype(jnp.float32)  53.3 us
    reduce_scatter x1, waiting for transfers between devices, shards(): lax.psum_scatter(partial_sum, 'rep', scatter_dimension=0, tiled=True)  25.6 us
    all_gather x1, blocking collectives, shards(): lax.all_gather(upstream_share, 'rep', axis=0, tiled=True)  16.2 us
    all_gather x1, blocking collectives, shards(): lax.all_gather(hidden_share, 'rep', axis=0, tiled=True)  14.8 us
    dot_general x1, local copies, waits for them, and re-layouts, shards(): jnp.einsum('jkab,jkaf->jkbf', own_tiles, picked_up, preferred_element_typ...  12.8 us
    dot_general x1, matrix products, shards(): jnp.einsum('jkab,jkaf->jkbf', own_tiles, picked_up, preferred_element_typ...  11.6 us
  transfers between devices with their start and end apart: 6, of which 6 were waited for; matrix products, arithmetic and copies ran while one was open for 3% of the time, Pallas kernels for 0%

commit v1 on v0

--- a/solution.py
+++ b/solution.py
@@ -65,9 +65,30 @@
     )
     hidden_share, grad_part, upstream_share = (out_rows, grad_part, up_rows)
     weight_grad = lax.psum(grad_part, ("section", "rep")) * grad_scale
+
+    def meet_panels_in(mat):
+        fresh, v1, e_now = (lax.psum(1, axis_name="rep"), lax.axis_index("rep"), mat.shape[0])
+        grid = [(no, (no + 1) % fresh) for no in range(fresh)]
+        buffer = [(no, (no - 1) % fresh) for no in range(fresh)]
+        e_next = jnp.zeros((*mat.shape[:0], fresh * e_now, *mat.shape[1:]), mat.dtype)
+        e_next = lax.dynamic_update_slice_in_dim(e_next, mat, v1 * e_now, axis=0)
+        right_arr = y1 = mat
+        reply = fresh // 2
+        for d in range(1, reply + 1):
+            right_arr = lax.ppermute(right_arr, axis_name="rep", perm=grid)
+            e_next = lax.dynamic_update_slice_in_dim(
+                e_next, right_arr, (v1 - d) % fresh * e_now, axis=0
+            )
+            if d < fresh - reply:
+                y1 = lax.ppermute(y1, axis_name="rep", perm=buffer)
+                e_next = lax.dynamic_update_slice_in_dim(
+                    e_next, y1, (v1 + d) % fresh * e_now, axis=0
+                )
+        return e_next
+
     hidden, upstream = (
         lax.all_gather(hidden_share, "rep", axis=0, tiled=True),
-        lax.all_gather(upstream_share, "rep", axis=0, tiled=True),
+        meet_panels_in(upstream_share),
     )
     up_blocks = upstream.reshape(blocks, block_rows, width)
     picked_up = jnp.take(up_blocks, row_table.reshape(-1), axis=0).reshape(

time: 488 us -> 486 us (level)
  blocking collectives: 31 us -> 14.8 us
  waiting for transfers between devices: 338 us -> 349 us
    all_gather x1 -> x0, blocking collectives: 16.2 us -> none  [shards(): lax.all_gather(upstream_share, 'rep', axis=0, tiled=True)]
    ppermute x0 -> x3, waiting for transfers between devices: none -> 10.3 us  [the longest x2 10 us: meet_panels_in(): right_arr = lax.ppermute(right_arr, axis_name='rep', perm=grid)]
  transfers between devices with their start and end apart: 6 -> 9, of which waited for: 6 -> 9; matrix products, arithmetic and copies ran while one was open for 3% -> 3% of each run, Pallas kernels for 0% -> 0%
where the time goes in v1:
time: 486 us
  waiting for transfers between devices  349 us (72%)
  local copies, waits for them, and re-layouts  49.3 us (10%)
  matrix products  40.4 us (8%)
  between operations  15.8 us (3%)
  blocking collectives  14.8 us (3%)
  other arithmetic  12.4 us (3%)
    psum x3, waiting for transfers between devices, spread(): return lax.psum(kept, axis)  152 us
    psum x1, waiting for transfers between devices, shards(): weight_grad = lax.psum(grad_part, ('section', 'rep')) * grad_scale  107 us
    psum x1, waiting for transfers between devices, shards(): lax.psum(contrib.astype(jnp.bfloat16), 'section').astype(jnp.float32)  53.3 us
    reduce_scatter x1, waiting for transfers between devices, shards(): lax.psum_scatter(partial_sum, 'rep', scatter_dimension=0, tiled=True)  26.4 us
    all_gather x1, blocking collectives, shards(): lax.all_gather(hidden_share, 'rep', axis=0, tiled=True)  14.8 us
    dot_general x1, local copies, waits for them, and re-layouts, shards(): jnp.einsum('jkab,jkaf->jkbf', own_tiles, picked_up, preferred_element_typ...  12.7 us
    dot_general x1, matrix products, shards(): jnp.einsum('jkab,jkaf->jkbf', own_tiles, picked_up, preferred_element_typ...  11.6 us
    dot_general x2, matrix products, forward_round(): jnp.einsum('pk,kaf->paf', select, products, precision=lax.Precision.HIGHEST)  11.5 us
  transfers between devices with their start and end apart: 9, of which 9 were waited for; matrix products, arithmetic and copies ran while one was open for 3% of the time, Pallas kernels for 0%

profile of v1, /device:TPU:0, one launch (start us, length us, event | category | flops | bytes accessed | tf_op | source)
XLA Modules:
  0.0 485.8 jit_solution(8076504903771594842)
XLA Ops:
  8.0 0.8 compare_select_fusion.2
  8.8 0.7 compare_and_fusion.1
  9.5 6.2 %gather_fusion.1 = bf16[2048,128]{1,0:T(8,128)(2,1)S(1)} fusion(bf16[2048,128]{1,0:T(8,128)(2,1)S(1)} %copy-done, s32[2048]{0:T(1024)S(1)} %get-tuple-element.296), kind=kCustom, calls=%fused_computation.1 | custom fusion | bytes 1056768 | tf_op jit(solution)/shard_map/jit(_take)/gather | solution.py:30
  15.7 0.3 broadcast_select_fusion.1
  16.0 147.5 %while.16 = (s32[]{:T(128)}, f32[16,128,128]{2,0,1:T(8,128)S(1)}, s32[2,96]{1,0:T(2,128)}, s32[2]{0:T(128)}, bf16[2,96,128,128]{3,2,1,0:T(8,128)(2,1)}, /*index=...) while((s32[]{:T(128)}, f32[16,128,128]{2,0,1:T(8,128)S(1)}, ...), condition=%wide.region_2.3_spmd.clone, body=%wide.region_0.0_spmd.clone.sunk | while | flops 707269568 | bytes 31465112 | solution.py:48
  16.0 0.0 all-reduce.11.cloned.1.call-start
  16.1 0.8 broadcast_select_fusion.3
  16.9 0.0 all-reduce.11.cloned.1.call-update
  17.0 0.7 fusion.64
  17.7 0.7 compare_and_fusion.4
  18.3 1.2 dynamic_slice.80
  19.6 0.6 iota_compare_fusion.5
  20.2 0.7 fusion.66
  20.9 57.2 %all-reduce.11.cloned.1.call-done = bf16[16,128,128]{2,1,0:T(8,128)(2,1)} async-done(((bf16[16,128,128]{2,1,0:T(8,128)(2,1)}), bf16[16,128,128]{2,1,0:T(8,128)(2,1)}) %all-reduce.11.cloned.1.call-update) | async-done | bytes 524304 | tf_op jit(solution)/shard_map/while/body/eval_jaxpr/psum | solution.py:10
  78.1 3.7 gather_fusion
  81.9 3.9 fusion.65
  85.8 5.7 %fusion.67 = f32[16,128,128]{2,0,1:T(8,128)S(1)} fusion(f32[96,128,128]{2,1,0:T(8,128)S(1)} %fusion.65, f32[16,128,128]{2,0,1:T(8,128)S(1)} %get-tuple-element.362, pred[]{:T(512)S(6)} %compare.9, s32[96]{0:T(128)S(1)} %fusion.66, pred[96]{0:T(512)(128)(4,1)S(1)} %iota_compare_fusion.5), kind=kOutput, calls=%fused_computation.14.clone.1 | convolution fusion | flops 302517248 | bytes 8389089 | tf_op jit(solution)/shard_map/while/body/eval_jaxpr/pk,kaf->paf/dot_general | solution.py:44
  91.5 0.0 all-reduce.11.cloned.1.call-start
  91.6 0.8 broadcast_select_fusion.3
  92.4 0.0 all-reduce.11.cloned.1.call-update
  92.4 0.7 fusion.64
  93.1 0.7 compare_and_fusion.4
  93.8 1.2 dynamic_slice.80
  95.0 0.6 iota_compare_fusion.5
  95.7 0.7 fusion.66
  96.4 53.8 %all-reduce.11.cloned.1.call-done = bf16[16,128,128]{2,1,0:T(8,128)(2,1)} async-done(((bf16[16,128,128]{2,1,0:T(8,128)(2,1)}), bf16[16,128,128]{2,1,0:T(8,128)(2,1)}) %all-reduce.11.cloned.1.call-update) | async-done | bytes 524304 | tf_op jit(solution)/shard_map/while/body/eval_jaxpr/psum | solution.py:10
  150.2 3.7 gather_fusion
  153.9 3.9 fusion.65
  157.8 5.7 %fusion.67 = f32[16,128,128]{2,0,1:T(8,128)S(1)} fusion(f32[96,128,128]{2,1,0:T(8,128)S(1)} %fusion.65, f32[16,128,128]{2,0,1:T(8,128)S(1)} %get-tuple-element.362, pred[]{:T(512)S(6)} %compare.9, s32[96]{0:T(128)S(1)} %fusion.66, pred[96]{0:T(512)(128)(4,1)S(1)} %iota_compare_fusion.5), kind=kOutput, calls=%fused_computation.14.clone.1 | convolution fusion | flops 302517248 | bytes 8389089 | tf_op jit(solution)/shard_map/while/body/eval_jaxpr/pk,kaf->paf/dot_general | solution.py:44
  163.6 0.0 reduce-scatter.2.cloned.1.call-start
  163.6 1.3 copy.11
  164.9 0.0 reduce-scatter.2.cloned.1.call-update
  164.9 0.0 all-reduce.7.cloned.1.call-start
  165.0 0.8 reshape_squeeze.3
  165.8 0.7 compare_and_fusion.2
  166.4 26.4 %reduce-scatter.2.cloned.1.call-done = f32[512,128]{1,0:T(8,128)} async-done(((f32[2048,128]{1,0:T(8,128)}), f32[512,128]{1,0:T(8,128)}) %reduce-scatter.2.cloned.1.call-update) | async-done | bytes 262160 | tf_op jit(solution)/shard_map/reduce_scatter | solution.py:53
  192.8 1.3 multiply_convert_fusion
  194.1 0.1 broadcast.124
  194.2 0.2 constant_dynamic-update-slice_fusion.3
  194.4 0.1 collective-permute-start
  194.5 0.7 iota_compare_fusion.3
  195.2 3.8 collective-permute-start.1
  199.0 3.6 collective-permute-done
  202.6 0.3 collective-permute-done.1
  202.9 6.4 %collective-permute-done.2 = bf16[512,128]{1,0:T(8,128)(2,1)S(1)} collective-permute-done((bf16[512,128]{1,0:T(8,128)(2,1)S(1)}, bf16[512,128]{1,0:T(8,128)(2,1)S(1)}, u32[]{:S(2)}, u32[]{:S(2)}) %collective-permute-start.2) | collective-permute-done | bytes 131104 | tf_op jit(solution)/shard_map/ppermute | solution.py:78
  209.4 8.0 %gather_fusion.2 = bf16[192,128,128]{2,1,0:T(8,128)(2,1)} fusion(bf16[16,128,128]{2,1,0:T(8,128)(2,1)S(1)} %bitcast.60, s32[1024]{0:T(1024)S(1)} %pad_clamp_fusion.1), kind=kCustom, calls=%fused_computation.2 | custom fusion | bytes 12583680 | tf_op jit(solution)/shard_map/jit(_take)/gather | solution.py:94
  217.4 11.6 %fusion.26 = f32[2,96,128,128]{3,2,1,0:T(8,128)} fusion(bf16[2,96,128,128]{3,2,1,0:T(8,128)(2,1)} %bitcast.64, pred[2,96]{1,0:T(4,128)(4,1)S(1)} %compare_and_fusion.2, bf16[1,1,2,96,128,128]{5,4,3,2,1,0:T(8,128)(2,1)} %bitcast.62), kind=kOutput, calls=%fused_computation.34 | convolution fusion | flops 808452096 | bytes 25166016 | tf_op jit(solution)/shard_map/jkab,jkaf->jkbf/dot_general | solution.py:97
  228.9 12.7 %copy.14 = f32[2,96,128,128]{2,1,3,0:T(8,128)} copy(f32[2,96,128,128]{3,2,1,0:T(8,128)} %fusion.26) | data formatting | bytes 25165824 | tf_op jit(solution)/shard_map/jkab,jkaf->jkbf/dot_general | solution.py:97
  241.6 7.2 %fusion.30 = bf16[2,16,128,128]{3,1,2,0:T(8,128)(2,1)S(1)} fusion(f32[2,96,128,128]{2,1,3,0:T(8,128)} %copy.14, s32[2,96]{1,0:T(2,128)S(1)} %copy-done.3, pred[2,96]{1,0:T(4,128)(4,1)S(1)} %iota_compare_fusion.3), kind=kOutput, calls=%fused_computation.38 | convolution fusion | flops 604510208 | bytes 13632448 | tf_op jit(solution)/shard_map/jpk,jkbf->jpbf/dot_general | solution.py:104
  248.9 1.3 copy.12
  250.1 0.0 all-reduce.7.cloned.1.call-update
  250.2 0.0 all-reduce.5.cloned.1.call-start
  250.3 0.9 fusion.37
  251.1 0.0 all-reduce.5.cloned.1.call-update
  251.1 0.0 all-reduce.9.cloned.1.call-start
  251.2 53.3 %all-reduce.7.cloned.1.call-done = bf16[2,2048,128]{2,1,0:T(8,128)(2,1)} async-done(((bf16[2,2048,128]{2,1,0:T(8,128)(2,1)}), bf16[2,2048,128]{2,1,0:T(8,128)(2,1)}) %all-reduce.7.cloned.1.call-update) | async-done | bytes 1048592 | tf_op jit(solution)/shard_map/psum | solution.py:109
  304.5 1.9 fusion.34
  306.4 0.0 all-reduce.9.cloned.1.call-update
  306.4 14.8 %all_gather.3 = bf16[2048,128]{1,0:T(8,128)(2,1)S(1)} all-gather(bf16[512,128]{1,0:T(8,128)(2,1)S(1)} %get-tuple-element.294), channel_id=1, replica_groups=mesh['section'=8,'rep'=4] {'rep'}, dimensions={0}, use_global_device_ids=true | all-gather | bytes 655360 | tf_op jit(solution)/shard_map/all_gather | solution.py:90
  321.2 106.7 %all-reduce.5.cloned.1.call-done = f32[128,128]{1,0:T(8,128)} async-done(((f32[128,128]{1,0:T(8,128)}), f32[128,128]{1,0:T(8,128)}) %all-reduce.5.cloned.1.call-update) | async-done | bytes 65552 | tf_op jit(solution)/shard_map/psum | solution.py:67
  428.0 1.5 broadcast_multiply_fusion
  429.5 41.1 %all-reduce.9.cloned.1.call-done = bf16[2048,128]{1,0:T(8,128)(2,1)} async-done(((bf16[2048,128]{1,0:T(8,128)(2,1)}), bf16[2048,128]{1,0:T(8,128)(2,1)}) %all-reduce.9.cloned.1.call-update) | async-done | bytes 524304 | tf_op jit(solution)/shard_map/psum | solution.py:10
  470.5 6.8 %scatter_custom_fusion = bf16[2048,128]{1,0:T(8,128)(2,1)} fusion(s32[2048]{0:T(1024)S(1)} %get-tuple-element.295, bf16[2048,128]{1,0:T(8,128)(2,1)} %all-reduce.9.cloned.1.call-done, bf16[]{:T(256)} %constant.206.clone.1), kind=kCustom, calls=%fused_computation.44 | custom fusion | bytes 524800 | tf_op jit(solution)/shard_map/scatter | solution.py:114
  477.4 0.8 copy.37
  (17 shorter events, 0.1 us)
Async XLA Ops:
  8.0 1.5 copy-start
  16.0 176.8 %copy-start.2 = (bf16[128,128]{1,0:T(8,128)(2,1)S(1)}, bf16[128,128]{1,0:T(8,128)(2,1)}, u32[]{:S(2)}) copy-start(bf16[128,128]{1,0:T(8,128)(2,1)} %param.16) | copy-start | bytes 98308
  16.0 62.1 %all-reduce.11.cloned.1.call-start = ((), (), s32[]{:S(2)}) async-start(), calls=%async_computation.5 | async-start | bytes 1048576 | tf_op jit(solution)/shard_map/while/body/eval_jaxpr/psum | solution.py:10
  91.5 58.7 %all-reduce.11.cloned.1.call-start = ((), (), s32[]{:S(2)}) async-start(), calls=%async_computation.5 | async-start | bytes 1048576 | tf_op jit(solution)/shard_map/while/body/eval_jaxpr/psum | solution.py:10
  163.6 29.2 %reduce-scatter.2.cloned.1.call-start = ((), (), s32[]{:S(2)}) async-start(), calls=%async_computation.1 | async-start | bytes 1310720 | tf_op jit(solution)/shard_map/reduce_scatter | solution.py:53
  164.9 139.5 %all-reduce.7.cloned.1.call-start = ((), (), s32[]{:S(2)}) async-start(), calls=%async_computation.3 | async-start | bytes 2097152 | tf_op jit(solution)/shard_map/psum | solution.py:109
  194.4 8.2 %collective-permute-start = (bf16[512,128]{1,0:T(8,128)(2,1)S(1)}, bf16[512,128]{1,0:T(8,128)(2,1)S(1)}, u32[]{:S(2)}, u32[]{:S(2)}) collective-permute-start(bf16[512,128]{1,0:T(8,128)(2,1)S(1)} %get-tuple-element.298), channel_id=1, source_target_pairs={{0,1},{1,2},{2,3},{3,0},{4,5},{5,6},{6,7},{7,4},{8,9},{9,10},{10,1... | collective-permute-start | bytes 393224 | tf_op jit(solution)/shard_map/ppermute | solution.py:78
  195.2 7.7 %collective-permute-start.1 = (bf16[512,128]{1,0:T(8,128)(2,1)S(1)}, bf16[512,128]{1,0:T(8,128)(2,1)S(1)}, u32[]{:S(2)}, u32[]{:S(2)}) collective-permute-start(bf16[512,128]{1,0:T(8,128)(2,1)S(1)} %get-tuple-element.298), channel_id=1, source_target_pairs={{0,3},{1,0},{2,1},{3,2},{4,7},{5,4},{6,5},{7,6},{8,11},{9,8},{10,9... | collective-permute-start | bytes 393224 | tf_op jit(solution)/shard_map/ppermute | solution.py:83
  202.6 6.8 %collective-permute-start.2 = (bf16[512,128]{1,0:T(8,128)(2,1)S(1)}, bf16[512,128]{1,0:T(8,128)(2,1)S(1)}, u32[]{:S(2)}, u32[]{:S(2)}) collective-permute-start(bf16[512,128]{1,0:T(8,128)(2,1)S(1)} %collective-permute-done), channel_id=1, source_target_pairs={{0,1},{1,2},{2,3},{3,0},{4,5},{5,6},{6,7},{7,4},{8,9},{9,10},{10,1... | collective-permute-start | bytes 393224 | tf_op jit(solution)/shard_map/ppermute | solution.py:78
  228.9 12.7 %copy-start.3 = (s32[2,96]{1,0:T(2,128)S(1)}, s32[2,96]{1,0:T(2,128)}, u32[]{:S(2)}) copy-start(s32[2,96]{1,0:T(2,128)} %get-tuple-element.419) | copy-start | bytes 2308
  241.6 8.7 %copy-start.1 = (f32[512,128]{1,0:T(8,128)S(1)}, f32[512,128]{1,0:T(8,128)}, u32[]{:S(2)}) copy-start(f32[512,128]{1,0:T(8,128)} %reduce-scatter.2.cloned.1.call-done) | copy-start | bytes 786436
  250.2 177.8 %all-reduce.5.cloned.1.call-start = ((), (), s32[]{:S(2)}) async-start(), calls=%async_computation.2 | async-start | bytes 131072 | tf_op jit(solution)/shard_map/psum | solution.py:67
  251.1 219.4 %all-reduce.9.cloned.1.call-start = ((), (), s32[]{:S(2)}) async-start(), calls=%async_computation.4 | async-start | bytes 1048576 | tf_op jit(solution)/shard_map/psum | solution.py:10
Sparse Core Ops, SparseCore 0:
  20.8 57.2 all-reduce.10
  96.3 53.8 all-reduce.10
Sparse Core Ops, SparseCore 1:
  166.3 26.4 reduce-scatter.1
  250.3 54.2 all-reduce.6
  311.5 116.5 all-reduce.4
  431.0 39.4 all-reduce.8
